TPU v7x, 32 devices: a whole 2x2x4 slice. The times are simulated.
32 devices in a mesh: section: 8 (over z, x), dp: 4 (over y, core).
Axes of the slice: x: 2, y: 2, z: 4, core: 2. Of those that a mesh axis runs over, the one named last changes fastest.
Arguments:
- act_in: bfloat16 [8, 128, 2048], P('section', None, 'dp'), may hold values from -6 to 6
- saved_act: bfloat16 [8, 128, 2048], P('section', None, 'dp'), may hold values from -6 to 6
- cotangent: bfloat16 [8, 128, 2048], P('section', None, 'dp'), may hold values from -6 to 6
- weight_xz: bfloat16 [8, 2048, 8192], P('section', 'dp'), may hold values from -0.125 to 0.125
- weight_bcdt: bfloat16 [8, 320, 2048], P('section', None, 'dp'), may hold values from -0.125 to 0.125
- weight_out: bfloat16 [8, 4096, 2048], P('section', None, 'dp'), may hold values from -0.09375 to 0.09375
- conv_x: float32 [8, 4, 4096], P('section', None, 'dp'), may hold values from -3 to 3
- conv_bc: float32 [8, 4, 256], P('section'), may hold values from -3 to 3
- dt_bias: float32 [8, 64], P('section', 'dp'), may hold values from -8 to -2
- a_log: float32 [8, 64], P('section', 'dp'), may hold values from 0 to 2.7
- d_skip: float32 [8, 64], P('section', 'dp'), may hold values from 0.5 to 1.5
- norm_gain: float32 [8, 4096], P('section', 'dp'), may hold values from 0.1 to 1.9
Outputs:
- next_act: bfloat16 [8, 128, 2048], P('section', None, 'dp')
- prev_grad: bfloat16 [8, 128, 2048], P('section', None, 'dp')
- grad_xz: float32 [8, 2048, 8192], P('section', 'dp')
- grad_bcdt: float32 [8, 320, 2048], P('section', None, 'dp')
- grad_out: float32 [8, 4096, 2048], P('section', None, 'dp')
All inputs are finite; a program needn't handle non-finite values.
Results may differ from a plain program's by a relative error of at most 0.0084.
Values may be sent and summed in bfloat16 or wider, within the bound.
A program may use at most 128 MiB of HBM per device.

v0:
```python
import jax
import jax.numpy as jnp
from jax import lax
from jax.sharding import PartitionSpec as P

D = 2048
HEAD_DIM = 64
NSTATE = 128
HEADS = 64
SEQ = 128
INNER = 4096


def from_behind(x, axis, by):
    length = lax.axis_size(axis)
    return lax.ppermute(x, axis, [(i, (i + by) % length) for i in range(length)])


def causal_conv(values, kernel_taps):
    kernel = kernel_taps.shape[0]
    length = values.shape[1]
    padded = jnp.pad(values, ((0, 0), (kernel - 1, 0), (0, 0)))
    running = jnp.zeros_like(values)
    for offset in range(kernel):
        running = running + kernel_taps[offset] * padded[:, offset : offset + length]
    return running


def map_scores(maps):
    input_map = maps[:, :, :NSTATE]
    output_map = maps[:, :, NSTATE:]
    return lax.dot_general(
        output_map, input_map, (((2,), (2,)), ((0,), (0,))), preferred_element_type=jnp.float32
    )


def map_grads(d_scores, maps):
    values = maps.astype(jnp.float32)
    input_map = values[:, :, :NSTATE]
    output_map = values[:, :, NSTATE:]
    d_input = jnp.einsum("bts,btn->bsn", d_scores, output_map, precision=lax.Precision.HIGHEST)
    d_output = jnp.einsum("bts,bsn->btn", d_scores, input_map, precision=lax.Precision.HIGHEST)
    return jnp.concatenate([d_input, d_output], axis=2)


def mixer(proj_x, proj_z, proj_dt, scores, conv_taps, dt_offset, log_rate, skip_gain):
    batch, length, width = proj_x.shape
    nheads = dt_offset.shape[0]
    head_width = width // nheads
    xconv = jax.nn.silu(causal_conv(proj_x, conv_taps))
    steps = jax.nn.softplus(proj_dt + dt_offset)
    cumul = jnp.cumsum(steps * -jnp.exp(log_rate), axis=1)
    position = jnp.arange(length)
    causal = (position[:, None] >= position[None, :])[None, None]
    heads_cum = jnp.swapaxes(cumul, 1, 2)
    spread = heads_cum[:, :, :, None] - heads_cum[:, :, None, :]
    decay = jnp.where(causal, jnp.exp(jnp.where(causal, spread, 0.0)), 0.0)
    weights = decay * scores[:, None] * jnp.swapaxes(steps, 1, 2)[:, :, None, :]
    heads_in = xconv.reshape(batch, length, nheads, head_width)
    result = jnp.einsum("bhts,bshp->bthp", weights, heads_in, precision=lax.Precision.HIGHEST)
    result = result + skip_gain[None, None, :, None] * heads_in
    gate_in = jax.nn.silu(proj_z.reshape(batch, length, nheads, head_width))
    return (result * gate_in).reshape(batch * length, width)


def times_transposed(left, right):
    return lax.dot_general(
        left, right, (((1,), (1,)), ((), ())), preferred_element_type=jnp.float32
    )


def transposed_times(left, right):
    return lax.dot_general(
        left, right, (((0,), (0,)), ((), ())), preferred_element_type=jnp.float32
    )


def feature_sum(values):
    return lax.psum(jnp.sum(values, axis=1), "dp")


def gate_sum(values):
    return lax.psum(jnp.sum(values, axis=1), "dp")


def send_along(row_block, direction):
    return from_behind(row_block, "section", direction)


def per_device(
    act_in,
    saved_act,
    cotangent,
    weight_xz,
    weight_bcdt,
    weight_out,
    conv_x,
    conv_bc,
    dt_bias,
    a_log,
    d_skip,
    norm_gain,
):
    input_rows = act_in[0]
    saved_rows = saved_act[0]
    cot_rows = cotangent[0]
    local_xz = weight_xz[0]
    local_bcdt = weight_bcdt[0]
    local_out = weight_out[0]
    taps_x = conv_x[0]
    taps_bc = conv_bc[0]
    dt_offset = dt_bias[0]
    log_rate = a_log[0]
    skip_gain = d_skip[0]
    gain_local = norm_gain[0]
    own_heads = dt_offset.shape[0]
    head_first = lax.axis_index("dp") * own_heads
    map_cols = 2 * NSTATE

    def whole_act(pre_part):
        batches = pre_part.shape[0] // SEQ
        conv_in = pre_part.reshape(batches, SEQ, map_cols)
        return jax.nn.silu(causal_conv(conv_in, taps_bc)).reshape(pre_part.shape)

    def project(rows):
        values = rows.astype(jnp.float32)
        scales = lax.rsqrt(feature_sum(values * values)[:, None] / D + 1e-05)
        normed = (values * scales).astype(jnp.bfloat16)
        part_xz = jnp.dot(normed, local_xz, preferred_element_type=jnp.float32)
        part_bcdt = times_transposed(normed, local_bcdt)
        own_xz = lax.psum_scatter(part_xz, "dp", scatter_dimension=1, tiled=True)
        whole_cols = lax.psum(part_bcdt, "dp")
        pre_part = whole_cols[:, :map_cols]
        maps = whole_act(pre_part).astype(jnp.bfloat16)
        own_dt = lax.dynamic_slice_in_dim(whole_cols[:, map_cols:], head_first, own_heads, 1)
        return (values, normed, scales, own_xz, pre_part, maps, own_dt)

    def gate_parts(projected):
        own_xz = projected[3]
        maps = projected[5]
        own_dt = projected[6]
        batches = own_xz.shape[0] // SEQ
        width = own_heads * HEAD_DIM
        split_xz = own_xz.reshape(batches, SEQ, own_heads, 2, HEAD_DIM)
        mix_x = split_xz[:, :, :, 0].reshape(batches, SEQ, width)
        mix_z = split_xz[:, :, :, 1].reshape(batches, SEQ, width)
        maps_three = maps.reshape(batches, SEQ, map_cols)
        scores = map_scores(maps_three)

        def local_mix(in_x, in_z, in_dt, in_scores):
            return mixer(in_x, in_z, in_dt, in_scores, taps_x, dt_offset, log_rate, skip_gain)

        gated, mix_back = jax.vjp(
            local_mix, mix_x, mix_z, own_dt.reshape(batches, SEQ, own_heads), scores
        )
        inverse = lax.rsqrt(gate_sum(gated * gated)[:, None] / INNER + 1e-05)
        mixed_in = (gated * inverse * gain_local).astype(jnp.bfloat16)
        return (gated, mix_back, inverse, mixed_in, maps_three)

    forward_proj = project(input_rows)
    back_proj = project(saved_rows)
    forward_mixed = gate_parts(forward_proj)[3]
    mixed = jnp.dot(
        lax.all_gather(forward_mixed, "dp", axis=1, tiled=True),
        local_out,
        preferred_element_type=jnp.float32,
    )
    section_out = (input_rows.astype(jnp.float32) + mixed).astype(jnp.bfloat16)
    next_act = send_along(section_out, 1)
    values, normed, scales, own_xz, pre_part, maps, own_dt = back_proj
    gated, mix_back, inverse, mixed_in, maps_three = gate_parts(back_proj)
    row_count = values.shape[0]
    grad_out = transposed_times(lax.all_gather(mixed_in, "dp", axis=1, tiled=True), cot_rows)
    d_mixed = lax.psum_scatter(
        times_transposed(cot_rows, local_out), "dp", scatter_dimension=1, tiled=True
    )
    dots = gate_sum(d_mixed * gain_local * gated)
    d_gated = (
        inverse * gain_local * d_mixed
        - gated * (inverse * inverse * inverse) * dots[:, None] / INNER
    )
    d_px, d_pz, d_pdt, d_scores = mix_back(d_gated)
    d_maps = map_grads(d_scores, maps_three).reshape(row_count, map_cols)
    d_dt_full = lax.dynamic_update_slice_in_dim(
        jnp.zeros((row_count, HEADS), jnp.float32),
        d_pdt.reshape(row_count, own_heads),
        head_first,
        1,
    )
    map_part = jnp.concatenate([d_maps, d_dt_full], axis=1)
    summed = lax.psum(map_part, "dp")
    conv_out, conv_back = jax.vjp(whole_act, pre_part)
    d_pre = conv_back(summed[:, :map_cols])[0]
    round_bcdt = jnp.concatenate([d_pre, summed[:, map_cols:]], axis=1).astype(jnp.bfloat16)
    own_round = (
        jnp.stack(
            [
                d_px.reshape(row_count, own_heads, HEAD_DIM),
                d_pz.reshape(row_count, own_heads, HEAD_DIM),
            ],
            axis=2,
        )
        .reshape(row_count, own_heads * 2 * HEAD_DIM)
        .astype(jnp.bfloat16)
    )
    round_xz = lax.all_gather(own_round, "dp", axis=1, tiled=True)
    grad_xz = transposed_times(normed, round_xz)
    grad_bcdt = transposed_times(round_bcdt, normed)
    d_normed = times_transposed(round_xz, local_xz)
    d_normed = d_normed + jnp.dot(round_bcdt, local_bcdt, preferred_element_type=jnp.float32)
    inner_sum = feature_sum(d_normed * values)[:, None]
    d_norm_in = scales * d_normed - values * (scales * scales * scales) * inner_sum / D
    d_input = (cot_rows.astype(jnp.float32) + d_norm_in).astype(jnp.bfloat16)
    prev_grad = send_along(d_input, -1)
    return (next_act[None], prev_grad[None], grad_xz[None], grad_bcdt[None], grad_out[None])


def solution(mesh):
    return jax.shard_map(
        per_device,
        mesh=mesh,
        in_specs=(
            P("section", None, "dp"),
            P("section", None, "dp"),
            P("section", None, "dp"),
            P("section", "dp", None),
            P("section", None, "dp"),
            P("section", None, "dp"),
            P("section", None, "dp"),
            P("section", None, None),
            P("section", "dp"),
            P("section", "dp"),
            P("section", "dp"),
            P("section", "dp"),
        ),
        out_specs=(
            P("section", None, "dp"),
            P("section", None, "dp"),
            P("section", "dp", None),
            P("section", None, "dp"),
            P("section", None, "dp"),
        ),
        check_vma=False,
    )
```

profile of v0, /device:TPU:0, one launch (start us, length us, event | category | flops | bytes accessed | tf_op | source)
XLA Modules:
  0.0 311.2 jit_solution(6612498661934579519)
XLA Ops:
  8.3 8.4 %psum.66 = f32[128]{0:T(128)S(1)} all-reduce(f32[128]{0:T(128)S(1)} %fusion.86), channel_id=1, replica_groups=mesh['section'=8,'dp'=4] {'dp'}, use_global_device_ids=true, to_apply=%region_8.9 | all-reduce | flops 128 | bytes 1024 | tf_op jit(solution)/shard_map/psum | solution.py:79
  17.2 1.9 fusion.80
  19.2 6.8 %fusion.2 = f32[128,8192]{1,0:T(8,128)} fusion(bf16[1,512,8192]{2,1,0:T(8,128)(2,1)} %param.15, bf16[1,128,512]{2,1,0:T(8,128)(2,1)} %param.13, f32[128]{0:T(128)S(1)} %get-tuple-element.49), kind=kOutput, calls=%fused_computation.3 | convolution fusion | flops 1073938432 | bytes 12714496 | tf_op jit(solution)/shard_map/dot_general | solution.py:129
  26.9 5.0 %fusion.6 = f32[128,4096]{1,0:T(8,128)} fusion(bf16[1,4096,512]{2,1,0:T(8,128)(2,1)} %param.17, bf16[1,128,512]{2,1,0:T(8,128)(2,1)S(1)} %copy-done.5), kind=kOutput, calls=%fused_computation.8 | convolution fusion | flops 536870912 | bytes 6422528 | tf_op jit(solution)/shard_map/dot_general | solution.py:67
  32.2 19.0 %all-reduce.18.cloned.1.call-done = f32[128,320]{0,1:T(8,128)} async-done(((f32[128,320]{0,1:T(8,128)}), f32[128,320]{0,1:T(8,128)}) %all-reduce.18.cloned.1.call-update) | async-done | bytes 163856 | tf_op jit(solution)/shard_map/psum | solution.py:132
  53.3 1.9 multiply_convert_fusion.2
  55.4 43.6 %reduce-scatter.6.cloned.1.call-done = f32[128,2048]{1,0:T(8,128)} async-done(((f32[128,8192]{1,0:T(8,128)}), f32[128,2048]{1,0:T(8,128)}) %reduce-scatter.6.cloned.1.call-update) | async-done | bytes 1048592 | tf_op jit(solution)/shard_map/reduce_scatter | solution.py:131
  99.0 1.5 copy.55
  101.8 3.0 multiply_reduce_fusion.3
  104.8 1.2 copy.60
  106.1 27.5 %reduce-scatter.8.cloned.1.call-done = f32[128,1024]{1,0:T(8,128)} async-done(((f32[128,4096]{1,0:T(8,128)}), f32[128,1024]{1,0:T(8,128)}) %reduce-scatter.8.cloned.1.call-update) | async-done | bytes 524304 | tf_op jit(solution)/shard_map/reduce_scatter | solution.py:174
  134.7 5.8 %all-reduce.13 = (f32[128]{0:T(128)S(1)}, f32[128]{0:T(128)S(1)}, f32[128]{0:T(128)S(1)}) all-reduce(f32[128]{0:T(128)S(1)} %fusion.84, f32[128]{0:T(128)S(1)} %multiply_reduce_fusion.2, f32[128]{0:T(128)S(1)} %get-tuple-element.20), channel_id=1, replica_groups=mesh['section'=8,'dp'=4] {'dp'}, use_global_device_ids=true, to_apply=%region_1.0 | all-reduce | flops 384 | bytes 3072 | tf_op jit(solution)/shard_map/psum | solution.py:79
  140.5 6.7 %fusion.4 = f32[128,8192]{1,0:T(8,128)} fusion(bf16[1,512,8192]{2,1,0:T(8,128)(2,1)} %param.15, bf16[1,128,512]{2,1,0:T(8,128)(2,1)S(1)} %copy-done.3, f32[128]{0:T(128)S(1)} %add_rsqrt_fusion.3), kind=kOutput, calls=%fused_computation.5 | convolution fusion | flops 1073938432 | bytes 12714496 | tf_op jit(solution)/shard_map/dot_general | solution.py:129
  147.5 2.0 multiply_convert_fusion
  149.7 4.2 %fusion.32 = (f32[16,128]{1,0:T(8,128)S(1)}, f32[16,128]{1,0:T(8,128)S(1)}, f32[16,128]{1,0:T(8,128)}, f32[128,128]{1,0:T(8,128)S(1)}) fusion(f32[16,128]{1,0:T(8,128)S(1)} %get-tuple-element.37, f32[128,128]{1,0:T(8,128)S(1)} %fusion.125, f32[16,128]{1,0:T(8,128)S(1)} %copy.57, pred[128,128]{1,0:T(8,128)(4,1)S(1)} %iota_compare_fusion, ...), kind=kOutput, calls=%fused_computation.47 | convolution fusion | flops 205891584 | bytes 1769472 | tf_op jit(solution)/shard_map/transpose(jvp(bhts,bshp->bthp))/dot_general | solution.py:60
  157.2 1.7 fusion.82
  159.1 2.3 fusion.10
  161.7 31.3 %reduce-scatter.4.cloned.1.call-done = f32[128,2048]{1,0:T(8,128)} async-done(((f32[128,8192]{1,0:T(8,128)}), f32[128,2048]{1,0:T(8,128)}) %reduce-scatter.4.cloned.1.call-update) | async-done | bytes 1048592 | tf_op jit(solution)/shard_map/reduce_scatter | solution.py:131
  193.0 1.5 copy.49
  194.6 1.9 broadcast_multiply_fusion.1
  198.9 28.8 %all-reduce.20.cloned.1.call-done = (f32[128,320]{0,1:T(8,128)}, f32[128,320]{0,1:T(8,128)}) async-done(((f32[128,320]{0,1:T(8,128)}, f32[128,320]{0,1:T(8,128)}), (f32[128,320]{0,1:T(8,128)}, f32[128,320]{0,1:T(8,128)})) %all-reduce.20.cloned.1.call-update) | async-done | bytes 327696 | tf_op jit(solution)/shard_map/psum | solution.py:132
  233.2 3.3 %multiply_reduce_fusion.4 = (f32[128]{0:T(128)S(1)}, f32[1,128,16,64]{1,3,2,0:T(8,128)S(1)}) fusion(f32[1,128,16,2,64]{1,4,3,2,0:T(8,128)S(1)} %bitcast.276, f32[1,128,16,64]{1,3,2,0:T(8,128)} %bitcast.288, f32[16]{0:T(128)S(1)} %bitcast.320, f32[128,16,64]{0,2,1:T(8,128)} %bitcast.289, f32[16,128]{1,0:T(8,128)S(1)} %get-tuple-element.35, ...), kind=kOutput, calls=%fused_computation.94 | convolution fusion | flops 203816832 | bytes 2204672 | tf_op jit(solution)/shard_map/jvp(bhts,bshp->bthp)/dot_general | solution.py:60
  236.8 15.6 %all-gather.6.cloned.1.call-done = bf16[128,8192]{0,1:T(8,128)(2,1)} async-done(((bf16[128,2048]{0,1:T(8,128)(2,1)}), bf16[128,8192]{0,1:T(8,128)(2,1)}) %all-gather.6.cloned.1.call-update) | async-done | bytes 2097168 | tf_op jit(solution)/shard_map/all_gather | solution.py:206
  252.3 6.9 %fusion = f32[128,512]{1,0:T(8,128)S(1)} fusion(bf16[128,8192]{0,1:T(8,128)(2,1)} %all-gather.6.cloned.1.call-done, bf16[1,512,8192]{2,1,0:T(8,128)(2,1)} %param.15), kind=kOutput, calls=%fused_computation.1 | convolution fusion | flops 1073741824 | bytes 10747904 | tf_op jit(solution)/shard_map/dot_general | solution.py:67
  259.6 6.3 %all-reduce.12 = (f32[128]{0:T(128)S(1)}, f32[128]{0:T(128)S(1)}) all-reduce(f32[128]{0:T(128)S(1)} %get-tuple-element.53, f32[128]{0:T(128)S(1)} %get-tuple-element.55), channel_id=1, replica_groups=mesh['section'=8,'dp'=4] {'dp'}, use_global_device_ids=true, to_apply=%region_6.7 | all-reduce | flops 256 | bytes 2048 | tf_op jit(solution)/shard_map/psum | solution.py:83
  267.9 3.4 %all-gather.8.cloned.1.call-done = bf16[128,4096]{1,0:T(8,128)(2,1)} async-done(((bf16[128,1024]{1,0:T(8,128)(2,1)}), bf16[128,4096]{1,0:T(8,128)(2,1)}) %all-gather.8.cloned.1.call-update) | async-done | bytes 1048592 | tf_op jit(solution)/shard_map/all_gather | solution.py:173
  271.3 5.9 %convolution_bitcast_fusion.1 = f32[1,4096,512]{2,1,0:T(8,128)} fusion(bf16[128,4096]{1,0:T(8,128)(2,1)} %all-gather.8.cloned.1.call-done, bf16[1,128,512]{2,1,0:T(8,128)(2,1)S(1)} %copy-done.5), kind=kOutput, calls=%fused_computation.7 | convolution fusion | flops 536870912 | bytes 9568256 | tf_op jit(solution)/shard_map/dot_general | solution.py:73
  277.4 4.3 %collective-permute-start.1 = (bf16[128,512]{1,0:T(8,128)(2,1)S(1)}, bf16[128,512]{1,0:T(8,128)(2,1)S(1)}, u32[]{:S(2)}, u32[]{:S(2)}) collective-permute-start(bf16[128,512]{1,0:T(8,128)(2,1)S(1)} %fusion.91), channel_id=1, source_target_pairs={{0,28},{4,0},{8,4},{12,8},{16,12},{20,16},{24,20},{28,24},{1,29},{... | collective-permute-start | bytes 393224 | tf_op jit(solution)/shard_map/ppermute | solution.py:16
  281.7 8.0 %all-gather.4.cloned.1.call-done = bf16[128,4096]{1,0:T(8,128)(2,1)} async-done(((bf16[128,1024]{1,0:T(8,128)(2,1)}), bf16[128,4096]{1,0:T(8,128)(2,1)}) %all-gather.4.cloned.1.call-update) | async-done | bytes 1048592 | tf_op jit(solution)/shard_map/all_gather | solution.py:164
  289.7 3.2 %fusion.17 = bf16[128,512]{1,0:T(8,128)(2,1)S(1)} fusion(bf16[128,4096]{1,0:T(8,128)(2,1)} %all-gather.4.cloned.1.call-done, bf16[1,4096,512]{2,1,0:T(8,128)(2,1)} %param.17, bf16[1,128,512]{2,1,0:T(8,128)(2,1)S(1)} %copy-done.4), kind=kOutput, calls=%fused_computation.28 | convolution fusion | flops 537067520 | bytes 5505024 | tf_op jit(solution)/shard_map/dot_general | solution.py:163
  292.9 1.5 collective-permute-start
  294.4 8.6 %convolution_bitcast_fusion = f32[1,512,8192]{2,1,0:T(8,128)} fusion(bf16[128,8192]{0,1:T(8,128)(2,1)S(1)} %copy-done.1, bf16[1,128,512]{2,1,0:T(8,128)(2,1)S(1)} %copy-done.2, f32[128]{0:T(128)S(1)} %get-tuple-element.49), kind=kOutput, calls=%fused_computation | convolution fusion | flops 1073938432 | bytes 19005952 | tf_op jit(solution)/shard_map/dot_general | solution.py:73
  (131 shorter events, 23.6 us)
Async XLA Ops:
  7.2 10.1 %copy-start = (bf16[1,320,512]{2,1,0:T(8,128)(2,1)S(1)}, bf16[1,320,512]{2,1,0:T(8,128)(2,1)}, u32[]{:S(2)}) copy-start(bf16[1,320,512]{2,1,0:T(8,128)(2,1)} %param.16) | copy-start | bytes 983044
  7.2 44.0 %all-reduce.18.cloned.1.call-start = ((), (), s32[]{:S(2)}) async-start(), calls=%async_computation.6 | async-start | bytes 327680 | tf_op jit(solution)/shard_map/psum | solution.py:132
  19.2 79.8 %reduce-scatter.6.cloned.1.call-start = ((), (), s32[]{:S(2)}) async-start(), calls=%async_computation.5 | async-start | bytes 5242880 | tf_op jit(solution)/shard_map/reduce_scatter | solution.py:131
  26.1 25.9 %copy-start.19 = (f32[1,16]{1,0:T(1,128)S(1)}, f32[1,16]{1,0:T(1,128)}, u32[]{:S(2)}) copy-start(f32[1,16]{1,0:T(1,128)} %param.20) | copy-start | bytes 196
  26.1 107.5 %reduce-scatter.8.cloned.1.call-start = ((), (), s32[]{:S(2)}) async-start(), calls=%async_computation.7 | async-start | bytes 2621440 | tf_op jit(solution)/shard_map/reduce_scatter | solution.py:174
  31.9 69.9 %copy-start.27 = (f32[1,16]{1,0:T(1,128)S(1)}, f32[1,16]{1,0:T(1,128)}, u32[]{:S(2)}) copy-start(f32[1,16]{1,0:T(1,128)} %param.22) | copy-start | bytes 196
  31.9 161.1 %reduce-scatter.4.cloned.1.call-start = ((), (), s32[]{:S(2)}) async-start(), calls=%async_computation.3 | async-start | bytes 5242880 | tf_op jit(solution)/shard_map/reduce_scatter | solution.py:131
  32.1 21.2 %copy-start.21 = (f32[16]{0:T(128)}, f32[16]{0:T(128)S(1)}, u32[]{:S(2)}) copy-start(f32[16]{0:T(128)S(1)} %negate_bitcast_fusion) | copy-start | bytes 196
  32.2 68.4 %copy-start.13 = (f32[1,1,256]{2,1,0:T(1,128)}, f32[1,1,256]{2,1,0:T(1,128)S(1)}, u32[]{:S(2)}) copy-start(f32[1,1,256]{2,1,0:T(1,128)S(1)} %get-tuple-element.44) | copy-start | bytes 3076
  32.2 72.6 %copy-start.15 = (f32[1,1,256]{2,1,0:T(1,128)}, f32[1,1,256]{2,1,0:T(1,128)S(1)}, u32[]{:S(2)}) copy-start(f32[1,1,256]{2,1,0:T(1,128)S(1)} %get-tuple-element.46) | copy-start | bytes 3076
  52.0 97.6 %copy-start.17 = (f32[16,128]{1,0:T(8,128)}, f32[16,128]{1,0:T(8,128)S(1)}, u32[]{:S(2)}) copy-start(f32[16,128]{1,0:T(8,128)S(1)} %get-tuple-element.37) | copy-start | bytes 24580
  52.4 97.3 %copy-start.18 = (f32[16,128]{1,0:T(8,128)}, f32[16,128]{1,0:T(8,128)S(1)}, u32[]{:S(2)}) copy-start(f32[16,128]{1,0:T(8,128)S(1)} %copy.57) | copy-start | bytes 24580
  55.4 94.3 %copy-start.10 = (f32[128,128]{1,0:T(8,128)}, f32[128,128]{1,0:T(8,128)S(1)}, u32[]{:S(2)}) copy-start(f32[128,128]{1,0:T(8,128)S(1)} %fusion.125) | copy-start | bytes 196612
  100.6 33.0 %copy-start.11 = (f32[1,1024]{1,0:T(1,128)S(1)}, f32[1,1024]{1,0:T(1,128)}, u32[]{:S(2)}) copy-start(f32[1,1024]{1,0:T(1,128)} %param.23) | copy-start | bytes 12292
  101.8 45.4 %copy-start.8 = (f32[1,128,1024]{1,2,0:T(8,128)}, f32[1,128,1024]{1,2,0:T(8,128)S(1)}, u32[]{:S(2)}) copy-start(f32[1,128,1024]{1,2,0:T(8,128)S(1)} %get-tuple-element.24) | copy-start | bytes 1572868
  147.3 80.4 %all-reduce.20.cloned.1.call-start = ((), (), s32[]{:S(2)}) async-start(), calls=%async_computation.10 | async-start | bytes 655360 | tf_op jit(solution)/shard_map/psum | solution.py:132
  161.7 90.6 %all-gather.6.cloned.1.call-start = ((), (), s32[]{:S(2)}) async-start(), calls=%async_computation.8 | async-start | bytes 2621440 | tf_op jit(solution)/shard_map/all_gather | solution.py:206
  194.6 35.5 %copy-start.9 = (f32[1,128,256]{1,2,0:T(8,128)S(1)}, f32[1,128,256]{1,2,0:T(8,128)}, u32[]{:S(2)}) copy-start(f32[1,128,256]{1,2,0:T(8,128)} %get-tuple-element.23) | copy-start | bytes 393220
  194.6 36.5 %copy-start.14 = (f32[1,1,256]{2,1,0:T(1,128)S(1)}, f32[1,1,256]{2,1,0:T(1,128)}, u32[]{:S(2)}) copy-start(f32[1,1,256]{2,1,0:T(1,128)} %copy-done.13) | copy-start | bytes 3076
  194.6 36.5 %copy-start.16 = (f32[1,1,256]{2,1,0:T(1,128)S(1)}, f32[1,1,256]{2,1,0:T(1,128)}, u32[]{:S(2)}) copy-start(f32[1,1,256]{2,1,0:T(1,128)} %copy-done.15) | copy-start | bytes 3076
  196.5 36.1 %copy-start.20 = (f32[1,16]{1,0:T(1,128)S(1)}, f32[1,16]{1,0:T(1,128)}, u32[]{:S(2)}) copy-start(f32[1,16]{1,0:T(1,128)} %param.20) | copy-start | bytes 196
  196.5 36.1 %copy-start.22 = (f32[16]{0:T(128)S(1)}, f32[16]{0:T(128)}, u32[]{:S(2)}) copy-start(f32[16]{0:T(128)} %copy-done.21) | copy-start | bytes 196
  196.5 36.7 %copy-start.28 = (f32[1,16]{1,0:T(1,128)S(1)}, f32[1,16]{1,0:T(1,128)}, u32[]{:S(2)}) copy-start(f32[1,16]{1,0:T(1,128)} %param.22) | copy-start | bytes 196
  197.9 73.4 %all-gather.8.cloned.1.call-start = ((), (), s32[]{:S(2)}) async-start(), calls=%async_computation.9 | async-start | bytes 1310720 | tf_op jit(solution)/shard_map/all_gather | solution.py:173
  198.6 91.0 %all-gather.4.cloned.1.call-start = ((), (), s32[]{:S(2)}) async-start(), calls=%async_computation.4 | async-start | bytes 1310720 | tf_op jit(solution)/shard_map/all_gather | solution.py:164
  236.7 22.5 %copy-start.2 = (bf16[1,128,512]{2,1,0:T(8,128)(2,1)S(1)}, bf16[1,128,512]{2,1,0:T(8,128)(2,1)}, u32[]{:S(2)}) copy-start(bf16[1,128,512]{2,1,0:T(8,128)(2,1)} %param.13) | copy-start | bytes 393220
  267.9 9.3 %copy-start.6 = (bf16[1,128,512]{2,1,0:T(8,128)(2,1)S(1)}, bf16[1,128,512]{2,1,0:T(8,128)(2,1)}, u32[]{:S(2)}) copy-start(bf16[1,128,512]{2,1,0:T(8,128)(2,1)} %param.14) | copy-start | bytes 393220
  267.9 9.3 %copy-start.25 = (f32[128]{0:T(128)S(1)}, f32[128]{0:T(128)}, u32[]{:S(2)}) copy-start(f32[128]{0:T(128)} %get-tuple-element.48) | copy-start | bytes 1540
  267.9 21.8 %copy-start.4 = (bf16[1,128,512]{2,1,0:T(8,128)(2,1)S(1)}, bf16[1,128,512]{2,1,0:T(8,128)(2,1)}, u32[]{:S(2)}) copy-start(bf16[1,128,512]{2,1,0:T(8,128)(2,1)} %param.12) | copy-start | bytes 393220
  277.2 17.2 %copy-start.1 = (bf16[128,8192]{0,1:T(8,128)(2,1)S(1)}, bf16[128,8192]{0,1:T(8,128)(2,1)}, u32[]{:S(2)}) copy-start(bf16[128,8192]{0,1:T(8,128)(2,1)} %all-gather.6.cloned.1.call-done) | copy-start | bytes 6291460
  277.4 25.7 %collective-permute-start.1 = (bf16[128,512]{1,0:T(8,128)(2,1)S(1)}, bf16[128,512]{1,0:T(8,128)(2,1)S(1)}, u32[]{:S(2)}, u32[]{:S(2)}) collective-permute-start(bf16[128,512]{1,0:T(8,128)(2,1)S(1)} %fusion.91), channel_id=1, source_target_pairs={{0,28},{4,0},{8,4},{12,8},{16,12},{20,16},{24,20},{28,24},{1,29},{... | collective-permute-start | bytes 393224 | tf_op jit(solution)/shard_map/ppermute | solution.py:16
  292.9 10.1 %collective-permute-start = (bf16[128,512]{1,0:T(8,128)(2,1)S(1)}, bf16[128,512]{1,0:T(8,128)(2,1)S(1)}, u32[]{:S(2)}, u32[]{:S(2)}) collective-permute-start(bf16[128,512]{1,0:T(8,128)(2,1)S(1)} %fusion.17), channel_id=1, source_target_pairs={{0,4},{4,8},{8,12},{12,16},{16,20},{20,24},{24,28},{28,0},{1,5},{5... | collective-permute-start | bytes 393224 | tf_op jit(solution)/shard_map/ppermute | solution.py:16
  (7 other events, 41.0 us)
Sparse Core Ops, SparseCore 0:
  19.3 31.8 all-reduce.17
  54.4 44.5 reduce-scatter.5
  102.1 31.4 reduce-scatter.7
  147.4 45.5 reduce-scatter.3
  195.2 32.4 all-reduce.19
  229.7 22.5 all-gather.5
  254.4 16.8 all-gather.7
  272.9 16.7 all-gather.3
where the time goes:
time: 312 us; the launch traced here: 311 us
  waiting for transfers between devices  178 us (57%)
  matrix products  61.8 us (20%)
  blocking collectives  20.4 us (7%)
  other arithmetic  17.4 us (6%)
  between operations  14.7 us (5%)
  local copies, waits for them, and re-layouts  12.5 us (4%)
  starting transfers between devices  6.58 us (2%)
    reduce_scatter x2, waiting for transfers between devices, project(): own_xz = lax.psum_scatter(part_xz, 'dp', scatter_dimension=1, tiled=True)  74.9 us
    psum x2, waiting for transfers between devices, project(): whole_cols = lax.psum(part_bcdt, 'dp')  47.7 us
    reduce_scatter x1, waiting for transfers between devices, per_device(): lax.psum_scatter(times_transposed(cot_rows, local_out), 'dp', scatter_dim...  27.5 us
    dot_general x3, matrix products, transposed_times(): lax.dot_general(left, right, (((0,), (0,)), ((), ())), preferred_element_...  15.6 us
    all_gather x1, waiting for transfers between devices, per_device(): round_xz = lax.all_gather(own_round, 'dp', axis=1, tiled=True)  15.6 us
    dot_general x4, matrix products, times_transposed(): lax.dot_general(left, right, (((1,), (1,)), ((), ())), preferred_element_...  15.5 us
    psum x2, blocking collectives, feature_sum(): return lax.psum(jnp.sum(values, axis=1), 'dp')  14.1 us
    dot_general x2, matrix products, project(): part_xz = jnp.dot(normed, local_xz, preferred_element_type=jnp.float32)  13.5 us
  transfers between devices with their start and end apart: 10, of which 8 were waited for; matrix products, arithmetic and copies ran while one was open for 25% of the time, Pallas kernels for 0%

commit v1 on v0

--- a/solution.py
+++ b/solution.py
@@ -9,6 +9,12 @@
 HEADS = 64
 SEQ = 128
 INNER = 4096
+
+
+def gather_and_add(array, name):
+    terms = lax.all_gather(array, name, axis=0, tiled=False)
+    total = terms.sum(axis=0)
+    return total
 
 
 def from_behind(x, axis, by):
@@ -76,7 +82,7 @@
 
 
 def feature_sum(values):
-    return lax.psum(jnp.sum(values, axis=1), "dp")
+    return gather_and_add(jnp.sum(values, axis=1), "dp")
 
 
 def gate_sum(values):

time: 312 us -> 336 us (1.077)
  waiting for transfers between devices: 178 us -> 196 us
    psum x2 -> x1, waiting for transfers between devices: 47.7 us -> 13.5 us  [project(): whole_cols = lax.psum(part_bcdt, 'dp')]
    psum x0 -> x1, waiting for transfers between devices: none -> 27.6 us  [per_device(): summed = lax.psum(map_part, 'dp')]
    all_gather x0 -> x3, blocking collectives: none -> 16.3 us  [gather_and_add(): terms = lax.all_gather(array, name, axis=0, tiled=False)]
    psum x2 -> x0, blocking collectives: 14.1 us -> none  [feature_sum(): return lax.psum(jnp.sum(values, axis=1), 'dp')]
    reduce_scatter x2, waiting for transfers between devices: 74.9 us -> 86.4 us  [project(): own_xz = lax.psum_scatter(part_xz, 'dp', scatter_dimension=1, tiled=True)]
    all_gather x1, waiting for transfers between devices: 3.4 us -> 13.9 us  [per_device(): lax.all_gather(mixed_in, 'dp', axis=1, tiled=True)]
    reduce_scatter x1, waiting for transfers between devices: 27.5 us -> 19.5 us  [per_device(): lax.psum_scatter(times_transposed(cot_rows, local_out), 'dp', scatter_dim...]
    all_gather x1, waiting for transfers between devices: 7.98 us -> 14.9 us  [per_device(): lax.all_gather(forward_mixed, 'dp', axis=1, tiled=True)]
  transfers between devices with their start and end apart: 10 -> 10, of which waited for: 8 -> 8; matrix products, arithmetic and copies ran while one was open for 25% -> 20% of each run, Pallas kernels for 0% -> 0%
where the time goes in v1:
time: 336 us; the launch traced here: 335 us
  waiting for transfers between devices  196 us (58%)
  matrix products  64.1 us (19%)
  blocking collectives  22.9 us (7%)
  other arithmetic  16.2 us (5%)
  local copies, waits for them, and re-layouts  14.7 us (4%)
  between operations  14.7 us (4%)
  starting transfers between devices  6.35 us (2%)
    reduce_scatter x2, waiting for transfers between devices, project(): own_xz = lax.psum_scatter(part_xz, 'dp', scatter_dimension=1, tiled=True)  86.4 us
    psum x1, waiting for transfers between devices, per_device(): summed = lax.psum(map_part, 'dp')  27.6 us
    reduce_scatter x1, waiting for transfers between devices, per_device(): lax.psum_scatter(times_transposed(cot_rows, local_out), 'dp', scatter_dim...  19.5 us
    all_gather x1, waiting for transfers between devices, per_device(): round_xz = lax.all_gather(own_round, 'dp', axis=1, tiled=True)  18.9 us
    all_gather x3, blocking collectives, gather_and_add(): terms = lax.all_gather(array, name, axis=0, tiled=False)  16.3 us
    dot_general x4, matrix products, times_transposed(): lax.dot_general(left, right, (((1,), (1,)), ((), ())), preferred_element_...  15.9 us
    dot_general x3, matrix products, transposed_times(): lax.dot_general(left, right, (((0,), (0,)), ((), ())), preferred_element_...  15.6 us
    all_gather x1, waiting for transfers between devices, per_device(): lax.all_gather(forward_mixed, 'dp', axis=1, tiled=True)  14.9 us
  transfers between devices with their start and end apart: 10, of which 8 were waited for; matrix products, arithmetic and copies ran while one was open for 20% of the time, Pallas kernels for 0%

profile of v1, /device:TPU:0, one launch (start us, length us, event | category | flops | bytes accessed | tf_op | source)
XLA Modules:
  0.0 334.9 jit_solution(3692360902541815660)
XLA Ops:
  8.3 6.0 %all-gather.4 = f32[4,1,128]{2,1,0:T(1,128)S(1)} all-gather(f32[1,1,128]{2,1,0:T(1,128)S(1)} %bitcast.318), channel_id=3, replica_groups=mesh['section'=8,'dp'=4] {'dp'}, dimensions={0}, use_global_device_ids=true | all-gather | bytes 2560 | tf_op jit(solution)/shard_map/all_gather | solution.py:15
  15.9 5.3 %all-gather.3 = f32[4,1,128]{2,1,0:T(1,128)S(1)} all-gather(f32[1,1,128]{2,1,0:T(1,128)S(1)} %bitcast.319), channel_id=2, replica_groups=mesh['section'=8,'dp'=4] {'dp'}, dimensions={0}, use_global_device_ids=true | all-gather | bytes 2560 | tf_op jit(solution)/shard_map/all_gather | solution.py:15
  21.3 1.9 fusion.82
  23.1 1.9 fusion.80
  25.1 6.8 %fusion.2 = f32[128,8192]{1,0:T(8,128)} fusion(bf16[1,512,8192]{2,1,0:T(8,128)(2,1)} %param.15, bf16[1,128,512]{2,1,0:T(8,128)(2,1)} %param.13, f32[128]{0:T(128)S(1)} %get-tuple-element.50), kind=kOutput, calls=%fused_computation.3 | convolution fusion | flops 1073938432 | bytes 12714496 | tf_op jit(solution)/shard_map/dot_general | solution.py:135
  32.8 6.7 %fusion.4 = f32[128,8192]{1,0:T(8,128)} fusion(bf16[1,512,8192]{2,1,0:T(8,128)(2,1)} %param.15, bf16[1,128,512]{2,1,0:T(8,128)(2,1)S(1)} %copy-done.3, f32[128]{0:T(128)S(1)} %add_rsqrt_fusion.3), kind=kOutput, calls=%fused_computation.5 | convolution fusion | flops 1073938432 | bytes 12714496 | tf_op jit(solution)/shard_map/dot_general | solution.py:135
  40.4 5.1 %fusion.6 = f32[128,4096]{1,0:T(8,128)} fusion(bf16[1,4096,512]{2,1,0:T(8,128)(2,1)} %param.17, bf16[1,128,512]{2,1,0:T(8,128)(2,1)S(1)} %copy-done.5), kind=kOutput, calls=%fused_computation.8 | convolution fusion | flops 536870912 | bytes 6422528 | tf_op jit(solution)/shard_map/dot_general | solution.py:73
  45.7 13.5 %all-reduce.19.cloned.1.call-done = (f32[128,320]{0,1:T(8,128)}, f32[128,320]{0,1:T(8,128)}) async-done(((f32[128,320]{0,1:T(8,128)}, f32[128,320]{0,1:T(8,128)}), (f32[128,320]{0,1:T(8,128)}, f32[128,320]{0,1:T(8,128)})) %all-reduce.19.cloned.1.call-update) | async-done | bytes 327696 | tf_op jit(solution)/shard_map/psum | solution.py:138
  64.2 1.4 multiply_convert_fusion.2
  66.7 40.2 %reduce-scatter.6.cloned.1.call-done = f32[128,2048]{1,0:T(8,128)} async-done(((f32[128,8192]{1,0:T(8,128)}), f32[128,2048]{1,0:T(8,128)}) %reduce-scatter.6.cloned.1.call-update) | async-done | bytes 1048592 | tf_op jit(solution)/shard_map/reduce_scatter | solution.py:137
  106.8 1.5 copy.55
  108.4 46.2 %reduce-scatter.4.cloned.1.call-done = f32[128,2048]{1,0:T(8,128)} async-done(((f32[128,8192]{1,0:T(8,128)}), f32[128,2048]{1,0:T(8,128)}) %reduce-scatter.4.cloned.1.call-update) | async-done | bytes 1048592 | tf_op jit(solution)/shard_map/reduce_scatter | solution.py:137
  154.7 1.5 copy.49
  156.3 2.4 fusion.63
  158.6 4.3 %multiply_reduce_fusion.3 = (f32[128]{0:T(128)}, f32[1,128,16,64]{1,3,2,0:T(8,128)}, f32[1,128,16,64]{1,3,2,0:T(8,128)}) fusion(f32[1,128,16,2,64]{1,4,3,2,0:T(8,128)S(1)} %bitcast.274, f32[1,128,16,64]{1,3,2,0:T(8,128)S(1)} %bitcast.287, f32[16]{0:T(128)} %bitcast.320, f32[128,16,64]{0,2,1:T(8,128)S(1)} %bitcast.286, f32[16,128]{1,0:T(8,128)} %get-tuple-element.33, ...), kind=kOutput, calls=%fused_computation.80 | convolution fusion | flops 203816832 | bytes 2728960 | tf_op jit(solution)/shard_map/jvp(bhts,bshp->bthp)/dot_general | solution.py:66
  164.2 4.8 %multiply_reduce_fusion.4 = (f32[128]{0:T(128)}, f32[1,128,16,64]{1,3,2,0:T(8,128)}) fusion(f32[1,128,16,2,64]{1,4,3,2,0:T(8,128)S(1)} %bitcast.279, f32[1,128,16,64]{1,3,2,0:T(8,128)} %bitcast.289, f32[16]{0:T(128)} %bitcast.321, f32[128,16,64]{0,2,1:T(8,128)} %bitcast.290, f32[16,128]{1,0:T(8,128)} %get-tuple-element.47, f32[128,128]{1,0:T(8,128)} %fusion.124, ...), kind=kOutput, calls=%fused_computation.94 | convolution fusion | flops 203816832 | bytes 2204672 | tf_op jit(solution)/shard_map/jvp(bhts,bshp->bthp)/dot_general | solution.py:66
  169.0 19.5 %reduce-scatter.8.cloned.1.call-done = f32[128,1024]{1,0:T(8,128)} async-done(((f32[128,4096]{1,0:T(8,128)}), f32[128,1024]{1,0:T(8,128)}) %reduce-scatter.8.cloned.1.call-update) | async-done | bytes 524304 | tf_op jit(solution)/shard_map/reduce_scatter | solution.py:180
  189.7 6.6 %all-reduce.12 = (f32[128]{0:T(128)S(1)}, f32[128]{0:T(128)}, f32[128]{0:T(128)S(1)}) all-reduce(f32[128]{0:T(128)} %get-tuple-element.54, f32[128]{0:T(128)S(1)} %multiply_reduce_fusion.2, f32[128]{0:T(128)} %get-tuple-element.18), channel_id=1, replica_groups=mesh['section'=8,'dp'=4] {'dp'}, use_global_device_ids=true, to_apply=%region_6.7 | all-reduce | flops 384 | bytes 3072 | tf_op jit(solution)/shard_map/psum | solution.py:89
  198.0 2.1 multiply_convert_fusion
  200.4 3.6 %fusion.32 = (f32[16,128]{1,0:T(8,128)S(1)}, f32[16,128]{1,0:T(8,128)S(1)}, f32[16,128]{1,0:T(8,128)S(1)}, f32[128,128]{1,0:T(8,128)S(1)}) fusion(f32[16,128]{1,0:T(8,128)} %get-tuple-element.33, f32[128,128]{1,0:T(8,128)S(1)} %fusion.125, f32[16,128]{1,0:T(8,128)} %copy.57, pred[128,128]{1,0:T(8,128)(4,1)S(1)} %iota_compare_fusion, ...), kind=kOutput, calls=%fused_computation.47 | convolution fusion | flops 205891584 | bytes 1769472 | tf_op jit(solution)/shard_map/transpose(jvp(bhts,bshp->bthp))/dot_general | solution.py:66
  208.0 1.4 fusion.10
  211.8 27.6 %all-reduce.17.cloned.1.call-done = f32[128,320]{0,1:T(8,128)} async-done(((f32[128,320]{0,1:T(8,128)}), f32[128,320]{0,1:T(8,128)}) %all-reduce.17.cloned.1.call-update) | async-done | bytes 163856 | tf_op jit(solution)/shard_map/psum | solution.py:197
  242.7 14.9 %all-gather.10.cloned.1.call-done = bf16[128,4096]{1,0:T(8,128)(2,1)} async-done(((bf16[128,1024]{1,0:T(8,128)(2,1)}), bf16[128,4096]{1,0:T(8,128)(2,1)}) %all-gather.10.cloned.1.call-update) | async-done | bytes 1048592 | tf_op jit(solution)/shard_map/all_gather | solution.py:170
  257.6 3.2 fusion.17
  260.8 1.7 collective-permute-start
  262.6 13.9 %all-gather.14.cloned.1.call-done = bf16[128,4096]{1,0:T(8,128)(2,1)} async-done(((bf16[128,1024]{1,0:T(8,128)(2,1)}), bf16[128,4096]{1,0:T(8,128)(2,1)}) %all-gather.14.cloned.1.call-update) | async-done | bytes 1048592 | tf_op jit(solution)/shard_map/all_gather | solution.py:179
  276.5 5.9 %convolution_bitcast_fusion.1 = f32[1,4096,512]{2,1,0:T(8,128)} fusion(bf16[128,4096]{1,0:T(8,128)(2,1)} %all-gather.14.cloned.1.call-done, bf16[1,128,512]{2,1,0:T(8,128)(2,1)S(1)} %copy-done.5), kind=kOutput, calls=%fused_computation.7 | convolution fusion | flops 536870912 | bytes 9568256 | tf_op jit(solution)/shard_map/dot_general | solution.py:79
  282.4 18.9 %all-gather.12.cloned.1.call-done = bf16[128,8192]{0,1:T(8,128)(2,1)} async-done(((bf16[128,2048]{0,1:T(8,128)(2,1)}), bf16[128,8192]{0,1:T(8,128)(2,1)}) %all-gather.12.cloned.1.call-update) | async-done | bytes 2097168 | tf_op jit(solution)/shard_map/all_gather | solution.py:212
  301.2 7.1 %fusion = f32[128,512]{1,0:T(8,128)S(1)} fusion(bf16[128,8192]{0,1:T(8,128)(2,1)} %all-gather.12.cloned.1.call-done, bf16[1,512,8192]{2,1,0:T(8,128)(2,1)} %param.15), kind=kOutput, calls=%fused_computation.1 | convolution fusion | flops 1073741824 | bytes 10747904 | tf_op jit(solution)/shard_map/dot_general | solution.py:73
  308.6 5.0 %all-gather.5 = f32[4,1,128]{2,1,0:T(1,128)S(1)} all-gather(f32[1,1,128]{2,1,0:T(1,128)S(1)} %bitcast.317), channel_id=4, replica_groups=mesh['section'=8,'dp'=4] {'dp'}, dimensions={0}, use_global_device_ids=true | all-gather | bytes 2560 | tf_op jit(solution)/shard_map/all_gather | solution.py:15
  313.9 4.3 %collective-permute-start.1 = (bf16[128,512]{1,0:T(8,128)(2,1)S(1)}, bf16[128,512]{1,0:T(8,128)(2,1)S(1)}, u32[]{:S(2)}, u32[]{:S(2)}) collective-permute-start(bf16[128,512]{1,0:T(8,128)(2,1)S(1)} %fusion.91), channel_id=1, source_target_pairs={{0,28},{4,0},{8,4},{12,8},{16,12},{20,16},{24,20},{28,24},{1,29},{... | collective-permute-start | bytes 393224 | tf_op jit(solution)/shard_map/ppermute | solution.py:22
  318.2 8.6 %convolution_bitcast_fusion = f32[1,512,8192]{2,1,0:T(8,128)} fusion(bf16[128,8192]{0,1:T(8,128)(2,1)S(1)} %copy-done.1, bf16[1,128,512]{2,1,0:T(8,128)(2,1)S(1)} %copy-done.2, f32[128]{0:T(128)S(1)} %copy-done.9), kind=kOutput, calls=%fused_computation | convolution fusion | flops 1073938432 | bytes 19005952 | tf_op jit(solution)/shard_map/dot_general | solution.py:79
  (126 shorter events, 26.5 us)
Async XLA Ops:
  7.2 14.1 %copy-start = (bf16[1,320,512]{2,1,0:T(8,128)(2,1)S(1)}, bf16[1,320,512]{2,1,0:T(8,128)(2,1)}, u32[]{:S(2)}) copy-start(bf16[1,320,512]{2,1,0:T(8,128)(2,1)} %param.16) | copy-start | bytes 983044
  7.2 52.0 %all-reduce.19.cloned.1.call-start = ((), (), s32[]{:S(2)}) async-start(), calls=%async_computation.10 | async-start | bytes 655360 | tf_op jit(solution)/shard_map/psum | solution.py:138
  14.9 226.6 %copy-start.8 = (f32[128]{0:T(128)}, f32[128]{0:T(128)S(1)}, u32[]{:S(2)}) copy-start(f32[128]{0:T(128)S(1)} %get-tuple-element.50) | copy-start | bytes 1540
  25.1 81.8 %reduce-scatter.6.cloned.1.call-start = ((), (), s32[]{:S(2)}) async-start(), calls=%async_computation.5 | async-start | bytes 5242880 | tf_op jit(solution)/shard_map/reduce_scatter | solution.py:137
  31.9 122.7 %reduce-scatter.4.cloned.1.call-start = ((), (), s32[]{:S(2)}) async-start(), calls=%async_computation.3 | async-start | bytes 5242880 | tf_op jit(solution)/shard_map/reduce_scatter | solution.py:137
  39.5 6.0 %copy-start.24 = (f32[1,16]{1,0:T(1,128)S(1)}, f32[1,16]{1,0:T(1,128)}, u32[]{:S(2)}) copy-start(f32[1,16]{1,0:T(1,128)} %param.21) | copy-start | bytes 196
  39.5 6.0 %copy-start.18 = (f32[1,4,256]{2,1,0:T(4,128)S(1)}, f32[1,4,256]{2,1,0:T(4,128)}, u32[]{:S(2)}) copy-start(f32[1,4,256]{2,1,0:T(4,128)} %param.19) | copy-start | bytes 12292
  39.6 6.1 %copy-start.11 = (f32[1,4,1024]{2,1,0:T(4,128)S(1)}, f32[1,4,1024]{2,1,0:T(4,128)}, u32[]{:S(2)}) copy-start(f32[1,4,1024]{2,1,0:T(4,128)} %param.18) | copy-start | bytes 49156
  39.6 21.1 %copy-start.19 = (f32[1,16]{1,0:T(1,128)S(1)}, f32[1,16]{1,0:T(1,128)}, u32[]{:S(2)}) copy-start(f32[1,16]{1,0:T(1,128)} %param.20) | copy-start | bytes 196
  39.6 148.9 %reduce-scatter.8.cloned.1.call-start = ((), (), s32[]{:S(2)}) async-start(), calls=%async_computation.6 | async-start | bytes 2621440 | tf_op jit(solution)/shard_map/reduce_scatter | solution.py:180
  45.5 193.9 %all-reduce.17.cloned.1.call-start = ((), (), s32[]{:S(2)}) async-start(), calls=%async_computation.8 | async-start | bytes 327680 | tf_op jit(solution)/shard_map/psum | solution.py:197
  45.6 20.0 %copy-start.21 = (f32[16]{0:T(128)}, f32[16]{0:T(128)S(1)}, u32[]{:S(2)}) copy-start(f32[16]{0:T(128)S(1)} %negate_bitcast_fusion) | copy-start | bytes 196
  45.6 20.0 %copy-start.14 = (f32[1,1,256]{2,1,0:T(1,128)}, f32[1,1,256]{2,1,0:T(1,128)S(1)}, u32[]{:S(2)}) copy-start(f32[1,1,256]{2,1,0:T(1,128)S(1)} %get-tuple-element.45) | copy-start | bytes 3076
  45.6 110.6 %copy-start.12 = (f32[1,1,256]{2,1,0:T(1,128)}, f32[1,1,256]{2,1,0:T(1,128)S(1)}, u32[]{:S(2)}) copy-start(f32[1,1,256]{2,1,0:T(1,128)S(1)} %get-tuple-element.46) | copy-start | bytes 3076
  158.6 4.3 %copy-start.7 = (f32[1,128,1024]{1,2,0:T(8,128)}, f32[1,128,1024]{1,2,0:T(8,128)S(1)}, u32[]{:S(2)}) copy-start(f32[1,128,1024]{1,2,0:T(8,128)S(1)} %get-tuple-element.22) | copy-start | bytes 1572868
  163.0 25.5 %copy-start.10 = (f32[1,1024]{1,0:T(1,128)S(1)}, f32[1,1024]{1,0:T(1,128)}, u32[]{:S(2)}) copy-start(f32[1,1024]{1,0:T(1,128)} %param.23) | copy-start | bytes 12292
  200.3 5.4 %copy-start.20 = (f32[1,16]{1,0:T(1,128)S(1)}, f32[1,16]{1,0:T(1,128)}, u32[]{:S(2)}) copy-start(f32[1,16]{1,0:T(1,128)} %param.20) | copy-start | bytes 196
  200.3 5.4 %copy-start.22 = (f32[16]{0:T(128)S(1)}, f32[16]{0:T(128)}, u32[]{:S(2)}) copy-start(f32[16]{0:T(128)} %copy-done.21) | copy-start | bytes 196
  200.3 7.6 %copy-start.16 = (f32[16,128]{1,0:T(8,128)S(1)}, f32[16,128]{1,0:T(8,128)}, u32[]{:S(2)}) copy-start(f32[16,128]{1,0:T(8,128)} %get-tuple-element.33) | copy-start | bytes 24580
  200.4 7.6 %copy-start.17 = (f32[16,128]{1,0:T(8,128)S(1)}, f32[16,128]{1,0:T(8,128)}, u32[]{:S(2)}) copy-start(f32[16,128]{1,0:T(8,128)} %copy.57) | copy-start | bytes 24580
  200.4 7.6 %copy-start.25 = (f32[1,16]{1,0:T(1,128)S(1)}, f32[1,16]{1,0:T(1,128)}, u32[]{:S(2)}) copy-start(f32[1,16]{1,0:T(1,128)} %param.22) | copy-start | bytes 196
  206.6 51.0 %all-gather.10.cloned.1.call-start = ((), (), s32[]{:S(2)}) async-start(), calls=%async_computation.4 | async-start | bytes 1310720 | tf_op jit(solution)/shard_map/all_gather | solution.py:170
  207.1 69.3 %all-gather.14.cloned.1.call-start = ((), (), s32[]{:S(2)}) async-start(), calls=%async_computation.9 | async-start | bytes 1310720 | tf_op jit(solution)/shard_map/all_gather | solution.py:179
  207.9 93.3 %all-gather.12.cloned.1.call-start = ((), (), s32[]{:S(2)}) async-start(), calls=%async_computation.7 | async-start | bytes 2621440 | tf_op jit(solution)/shard_map/all_gather | solution.py:212
  209.7 30.5 %copy-start.15 = (f32[1,1,256]{2,1,0:T(1,128)S(1)}, f32[1,1,256]{2,1,0:T(1,128)}, u32[]{:S(2)}) copy-start(f32[1,1,256]{2,1,0:T(1,128)} %copy-done.14) | copy-start | bytes 3076
  210.1 31.0 %copy-start.13 = (f32[1,1,256]{2,1,0:T(1,128)S(1)}, f32[1,1,256]{2,1,0:T(1,128)}, u32[]{:S(2)}) copy-start(f32[1,1,256]{2,1,0:T(1,128)} %copy-done.12) | copy-start | bytes 3076
  210.2 31.4 %copy-start.2 = (bf16[1,128,512]{2,1,0:T(8,128)(2,1)S(1)}, bf16[1,128,512]{2,1,0:T(8,128)(2,1)}, u32[]{:S(2)}) copy-start(bf16[1,128,512]{2,1,0:T(8,128)(2,1)} %param.13) | copy-start | bytes 393220
  260.8 21.6 %collective-permute-start = (bf16[128,512]{1,0:T(8,128)(2,1)S(1)}, bf16[128,512]{1,0:T(8,128)(2,1)S(1)}, u32[]{:S(2)}, u32[]{:S(2)}) collective-permute-start(bf16[128,512]{1,0:T(8,128)(2,1)S(1)} %fusion.17), channel_id=1, source_target_pairs={{0,4},{4,8},{8,12},{12,16},{16,20},{20,24},{24,28},{28,0},{1,5},{5... | collective-permute-start | bytes 393224 | tf_op jit(solution)/shard_map/ppermute | solution.py:22
  282.4 31.3 %copy-start.9 = (f32[128]{0:T(128)S(1)}, f32[128]{0:T(128)}, u32[]{:S(2)}) copy-start(f32[128]{0:T(128)} %copy-done.8) | copy-start | bytes 1540
  282.4 31.3 %copy-start.23 = (f32[128]{0:T(128)S(1)}, f32[128]{0:T(128)}, u32[]{:S(2)}) copy-start(f32[128]{0:T(128)} %get-tuple-element.49) | copy-start | bytes 1540
  301.2 16.9 %copy-start.1 = (bf16[128,8192]{0,1:T(8,128)(2,1)S(1)}, bf16[128,8192]{0,1:T(8,128)(2,1)}, u32[]{:S(2)}) copy-start(bf16[128,8192]{0,1:T(8,128)(2,1)} %all-gather.12.cloned.1.call-done) | copy-start | bytes 6291460
  313.9 12.9 %collective-permute-start.1 = (bf16[128,512]{1,0:T(8,128)(2,1)S(1)}, bf16[128,512]{1,0:T(8,128)(2,1)S(1)}, u32[]{:S(2)}, u32[]{:S(2)}) collective-permute-start(bf16[128,512]{1,0:T(8,128)(2,1)S(1)} %fusion.91), channel_id=1, source_target_pairs={{0,28},{4,0},{8,4},{12,8},{16,12},{20,16},{24,20},{28,24},{1,29},{... | collective-permute-start | bytes 393224 | tf_op jit(solution)/shard_map/ppermute | solution.py:22
  (4 other events, 6.6 us)
Sparse Core Ops, SparseCore 0:
  25.2 33.9 all-reduce.18
  62.3 44.5 reduce-scatter.5
  110.1 44.5 reduce-scatter.3
  157.0 31.4 reduce-scatter.7
  206.7 32.6 all-reduce.16
  240.8 16.7 all-gather.9
  259.7 16.7 all-gather.13
  278.6 22.5 all-gather.11
